TPU v7x, 32 devices: a whole 2x2x4 slice. The times are simulated.
32 devices in a mesh: dates: 2 (over y), ctx: 16 (over z, x, core).
Axes of the slice: x: 2, y: 2, z: 4, core: 2. Of those that a mesh axis runs over, the one named last changes fastest.
Arguments:
- queries: bfloat16 [16384, 2048], P(('dates', 'ctx')), parts along dimension 0, may hold values from -6 to 6
- key_projection_rows: bfloat16 [16384, 1024], P(('dates', 'ctx')), parts along dimension 0, may hold values from -6 to 6
- value_projection_rows: bfloat16 [16384, 1024], P(('dates', 'ctx')), parts along dimension 0, may hold values from -6 to 6
- query_gain: float32 [256], replicated, may hold values from 0.5 to 1.5
- key_norm_gain: float32 [256], replicated, may hold values from 0.5 to 1.5
- session_flags: int32 [16384], P(('dates', 'ctx')), parts along dimension 0, may hold values from 0 to 1, as said below
- valid_length: int32 [2], P('dates'), parts along dimension 0, may hold values from 7936 to 8192
Outputs:
- attended: bfloat16 [16384, 2048], P(('dates', 'ctx')), parts along dimension 0
There are 2 independent parts, one for each index of `dates`. A program takes and returns all parts, laid end to end along the dimension named above; an argument that names none is the same for every part. Nothing has to cross between parts.
Inputs may be any that keep to these rules, and one draw needn't show every extreme that they name: `session_flags`: a 1 marks the first tick of a session; tick 0 always begins one; the ticks of some devices hold no session start.
All inputs are finite; a program needn't handle non-finite values.
Results may differ from a plain program's by a relative error of at most 0.012.
Values may be sent and summed in bfloat16 or wider, within the bound.
A program may use at most 128 MiB of HBM per device.

v0:
```python
import jax
import jax.numpy as jnp
from jax import lax
from jax.sharding import PartitionSpec as P

QUERY_HEADS = 8
KEY_VALUE_HEADS = 4
HEAD_DIMENSION = 256
WINDOW_TICKS = 1024


def shifted(array, axis, by):
    length = lax.axis_size(axis)
    pairs = [(i, i + by) for i in range(length) if 0 <= i + by < length]
    return lax.ppermute(array, axis, pairs)


def prefix(part, axis, combine, identity):
    place = lax.axis_index(axis)
    gathered = lax.all_gather(part, axis)
    state = jnp.zeros_like(part) + jnp.asarray(identity, part.dtype)

    def one(lap, state):
        return combine(state, lax.dynamic_index_in_dim(gathered, lap, 0, False))

    return lax.fori_loop(0, place, one, state)


def rootmean_rotary(inputs, gain, tick_positions, heads):
    grand_total = inputs.shape[0]
    vectors = inputs.astype(jnp.float32).reshape(grand_total, heads, HEAD_DIMENSION)
    vectors = (
        vectors * lax.rsqrt(jnp.mean(vectors * vectors, axis=-1, keepdims=True) + 1e-06) * gain
    )
    half_width = HEAD_DIMENSION // 2
    inverse = 10000.0 ** (-(jnp.arange(half_width, dtype=jnp.float32) * (2.0 / HEAD_DIMENSION)))
    angles = tick_positions.astype(jnp.float32)[:, None, None] * inverse
    cosine = jnp.cos(angles)
    sine = jnp.sin(angles)
    first = vectors[..., :half_width]
    second = vectors[..., half_width:]
    return jnp.concatenate(
        [first * cosine - second * sine, second * cosine + first * sine], axis=-1
    ).astype(jnp.bfloat16)


def attend(query_tile_block, key_tile_block, value_tile_block, query_pos, key_pos, starts, limit):
    block_extent = query_tile_block.shape[0]
    key_window_span = key_tile_block.shape[0]
    grouped_heads = query_tile_block.reshape(
        block_extent, KEY_VALUE_HEADS, QUERY_HEADS // KEY_VALUE_HEADS, HEAD_DIMENSION
    )
    key_head_split = key_tile_block.reshape(key_window_span, KEY_VALUE_HEADS, HEAD_DIMENSION)
    value_head_split = value_tile_block.reshape(key_window_span, KEY_VALUE_HEADS, HEAD_DIMENSION)
    scores = jnp.einsum(
        "qhgd,khd->hgqk", grouped_heads, key_head_split, preferred_element_type=jnp.float32
    ) * HEAD_DIMENSION ** (-0.5)
    allowed = (
        (key_pos[None, :] <= query_pos[:, None])
        & (key_pos[None, :] > query_pos[:, None] - WINDOW_TICKS)
        & (key_pos[None, :] >= starts[:, None])
    )
    weights = jnp.where(allowed, jnp.exp(scores), jnp.float32(0.0))
    totals = jnp.sum(weights, axis=-1)
    rounded = weights.astype(jnp.bfloat16)
    mixed = jnp.einsum(
        "hgqk,khd->qhgd", rounded, value_head_split, preferred_element_type=jnp.float32
    )
    mixed = mixed / jnp.transpose(totals, (2, 0, 1))[..., None]
    mixed = mixed.reshape(block_extent, QUERY_HEADS * HEAD_DIMENSION)
    mixed = jnp.where((query_pos < limit)[:, None], mixed, jnp.float32(0.0))
    return mixed.astype(jnp.bfloat16)


def body(
    queries,
    key_projection_rows,
    value_projection_rows,
    query_gain,
    key_norm_gain,
    session_flags,
    valid_length,
):
    partition_rows = queries.shape[0]
    hop_count = WINDOW_TICKS // partition_rows
    device_start = lax.axis_index("ctx") * partition_rows
    tick_positions = device_start + jnp.arange(partition_rows, dtype=jnp.int32)
    normed_q = rootmean_rotary(queries, query_gain, tick_positions, QUERY_HEADS).reshape(
        partition_rows, QUERY_HEADS * HEAD_DIMENSION
    )
    normalized_keys = rootmean_rotary(
        key_projection_rows, key_norm_gain, tick_positions, KEY_VALUE_HEADS
    ).reshape(partition_rows, KEY_VALUE_HEADS * HEAD_DIMENSION)
    marks = jnp.where(session_flags == 1, tick_positions, 0)
    payload = (normalized_keys, value_projection_rows)
    portions = [
        shifted((payload[0], payload[1]), "ctx", offset) for offset in range(hop_count, 0, -1)
    ]
    joined = tuple(
        (
            jnp.concatenate([portion[member] for portion in portions] + [payload[member]], axis=0)
            for member in range(len(payload))
        )
    )
    key_all = joined[0]
    value_all = joined[1]
    local_last = jnp.max(marks)
    prior = prefix(local_last, "ctx", jnp.maximum, jnp.zeros((), jnp.int32))
    starts = jnp.maximum(prior, lax.cummax(marks, axis=0))
    limit = valid_length[0]
    block_extent = min(partition_rows, 512)
    block_total = partition_rows // block_extent

    def one_block(block_index):
        first_row = block_index * block_extent
        query_pos = device_start + first_row + jnp.arange(block_extent, dtype=jnp.int32)
        key_pos = (
            device_start
            - WINDOW_TICKS
            + first_row
            + jnp.arange(WINDOW_TICKS + block_extent, dtype=jnp.int32)
        )
        return attend(normed_q, key_all, value_all, query_pos, key_pos, starts, limit)

    blocks = lax.map(one_block, jnp.arange(block_total, dtype=jnp.int32))
    return blocks.reshape(partition_rows, QUERY_HEADS * HEAD_DIMENSION)


def solution(mesh):
    in_specs = (
        P(("dates", "ctx"), None),
        P(("dates", "ctx"), None),
        P(("dates", "ctx"), None),
        P(),
        P(),
        P(("dates", "ctx")),
        P("dates"),
    )
    out_specs = P(("dates", "ctx"), None)
    return jax.shard_map(body, mesh=mesh, in_specs=in_specs, out_specs=out_specs, check_vma=False)
```

profile of v0, /device:TPU:27, one launch (start us, length us, event | category | flops | bytes accessed | tf_op | source)
XLA Modules:
  0.0 153.4 jit_solution(13460480409731498360)
XLA Ops:
  0.0 1.5 copy.32
  1.5 0.2 multiply_reduce_fusion.1
  1.8 0.5 copy.33
  2.3 0.7 fusion.22
  3.1 1.0 multiply_cosine_fusion
  4.1 0.3 multiply_multiply_fusion.1
  4.4 0.3 multiply_subtract_fusion
  4.8 0.5 copy.34
  5.4 1.3 collective-permute-start.2
  6.7 1.3 collective-permute-start.3
  8.0 1.3 collective-permute-start
  9.3 1.3 collective-permute-start.1
  10.6 0.3 reduce-window.9
  11.0 0.6 dynamic-slice
  11.6 1.4 dynamic-update-slice
  13.1 66.7 %all-reduce = s32[16]{0:T(128)S(1)} all-reduce(s32[16]{0:T(128)S(1)} %dynamic-update-slice), channel_id=1, replica_groups=mesh['dates'=2,'ctx'=16] {'ctx'}, use_global_device_ids=true, to_apply=%add | all-reduce | flops 16 | bytes 128
  79.8 21.0 %while.2 = (s32[]{:T(128)}, s32[]{:T(128)}, s32[]{:T(128)}, s32[16]{0:T(128)S(1)}, s32[]{:T(128)}, /*index=5*/s32[]{:T(128)}, s32[]{:T(128)}) while((s32[]{:T(128)}, s32[]{:T(128)}, s32[]{:T(128)}, s32[16]{0:T(128)S(1)}, s32[]{:T(128)}, /*index=5*/s32[]{:T(128)}, s32[]{:T(128)}) %tuple.27), condition=%wide.region_2.3_spmd, body=%wide.region_1.0_spmd.sunk | while | flops 6 | bytes 135 | solution.py:26
  79.8 0.7 dynamic_slice.8
  81.2 0.7 dynamic_slice.8
  82.6 0.7 dynamic_slice.8
  84.0 0.7 dynamic_slice.8
  85.4 0.7 dynamic_slice.8
  86.7 0.7 dynamic_slice.8
  88.1 0.7 dynamic_slice.8
  89.5 0.7 dynamic_slice.8
  90.9 0.7 dynamic_slice.8
  92.3 0.7 dynamic_slice.8
  93.7 0.7 dynamic_slice.8
  95.1 0.7 dynamic_slice.8
  96.5 0.7 dynamic_slice.8
  97.8 0.7 dynamic_slice.8
  99.2 0.7 dynamic_slice.8
  100.8 2.1 %copy.46 = f32[64,8,8,256]{3,2,1,0:T(8,128)S(1)} copy(bf16[64,8,8,256]{3,1,2,0:T(8,128)(2,1)} %bitcast.52) | data formatting | bytes 6291456
  102.9 1.9 %copy-done = f32[64,8,8,256]{3,2,1,0:T(8,128)} copy-done((f32[64,8,8,256]{3,2,1,0:T(8,128)}, f32[64,8,8,256]{3,2,1,0:T(8,128)S(1)}, u32[]{:S(2)}) %copy-start) | copy-done | bytes 4194328
  104.8 0.6 multiply_reduce_fusion
  105.7 2.6 %multiply_multiply_fusion = f32[512,8,256]{2,1,0:T(8,128)S(1)} fusion(f32[256]{0:T(256)S(1)} %copy-done.6, f32[512,8]{1,0:T(8,128)S(1)} %copy.38, f32[64,8,8,256]{3,2,1,0:T(8,128)} %copy-done), kind=kLoop, calls=%fused_computation.9 | loop fusion | flops 2097152 | bytes 8406016 | tf_op jit(solution)/shard_map/mul | solution.py:33
  108.3 0.6 subtract_convert_fusion
  108.9 1.2 copy.39
  110.1 1.1 copy.40
  112.1 1.9 %compare_and_fusion = pred[512,1536]{0,1:T(8,128)(4,1)} fusion(s32[512]{0:T(512)S(1)} %maximum_bitcast_fusion.2, s32[512]{0:T(512)S(1)} %get-tuple-element.72, s32[512]{0:T(512)S(1)} %get-tuple-element.71, s32[1536]{0:T(1024)S(1)} %iota_add_fusion), kind=kLoop, calls=%fused_computation.18 | loop fusion | flops 3932160 | bytes 798720 | tf_op jit(solution)/shard_map/while/body/eval_jaxpr/and | solution.py:59
  114.0 2.3 %copy.35 = bf16[512,4,256]{2,0,1:T(8,128)(2,1)} copy(bf16[512,4,256]{0,2,1:T(8,128)(2,1)} %bitcast.12) | data formatting | bytes 2097152 | tf_op jit(solution)/shard_map/concatenate | solution.py:101
  116.3 2.3 %copy.36 = bf16[512,4,256]{2,0,1:T(8,128)(2,1)} copy(bf16[512,4,256]{0,2,1:T(8,128)(2,1)} %bitcast.13) | data formatting | bytes 2097152 | tf_op jit(solution)/shard_map/concatenate | solution.py:101
  118.6 2.1 %pad_maximum_fusion = bf16[1536,1024]{1,0:T(8,128)(2,1)S(1)} fusion(bf16[512,1024]{1,0:T(8,128)(2,1)} %param.11, bf16[512,1024]{1,0:T(8,128)(2,1)} %collective-permute-done.1, bf16[512,1024]{1,0:T(8,128)(2,1)} %collective-permute-done), kind=kLoop, calls=%fused_computation.11 | loop fusion | flops 9437184 | bytes 6291456 | tf_op jit(solution)/shard_map/concatenate | solution.py:101
  120.7 3.0 %copy.31 = bf16[1536,1024]{0,1:T(8,128)(2,1)} copy(bf16[1536,1024]{1,0:T(8,128)(2,1)S(1)} %pad_maximum_fusion) | data formatting | bytes 6291456 | tf_op jit(solution)/shard_map/concatenate | solution.py:101
  123.7 13.3 %fusion = (f32[4,2,512]{2,1,0:T(2,128)S(1)}, f32[4,1536,512,2]{2,1,3,0:T(8,128)}) fusion(pred[512,1536]{0,1:T(8,128)(4,1)} %compare_and_fusion, bf16[512,4,2,128]{3,0,2,1:T(8,128)(2,1)} %bitcast.57, bf16[512,4,2,128]{3,0,2,1:T(8,128)(2,1)} %bitcast.56, bf16[512,4,256]{2,0,1:T(8,128)(2,1)} %copy-done.1, bf16[512,4,256]{2,0,1:T(8,128)(2,1)} %copy.36, ...), kind=kOutput, calls=%fused_computation.1 | convolution fusion | flops 3253727232 | bytes 31211520 | tf_op jit(solution)/shard_map/while/body/eval_jaxpr/qhgd,khd->hgqk/dot_general | solution.py:55
  137.0 11.7 %bitcast_divide_fusion = bf16[512,4,2,256]{0,3,2,1:T(8,128)(2,1)} fusion(bf16[1536,4,256,1]{0,2,3,1:T(8,128)(2,1)S(1)} %bitcast.51, f32[4,1536,512,2]{2,1,3,0:T(8,128)} %get-tuple-element.70, pred[512,1536]{0,1:T(8,128)(4,1)S(1)} %copy-done.3, f32[512,4,2]{0,2,1:T(2,128)S(1)} %bitcast.58), kind=kOutput, calls=%fused_computation.7 | convolution fusion | flops 3242196992 | bytes 31211520 | tf_op jit(solution)/shard_map/while/body/eval_jaxpr/hgqk,khd->qhgd/dot_general | solution.py:66
  148.7 2.9 %copy.42 = bf16[512,2048]{1,0:T(8,128)(2,1)S(1)} copy(bf16[512,2048]{0,1:T(8,128)(2,1)} %bitcast.53) | data formatting | bytes 4194304 | tf_op jit(solution)/shard_map/while/body/eval_jaxpr/reshape | solution.py:70
  151.7 1.7 %select_convert_fusion = bf16[512,2048]{1,0:T(8,128)(2,1)} fusion(bf16[512,2048]{1,0:T(8,128)(2,1)S(1)} %copy.42, pred[512]{0:T(512)(128)(4,1)S(1)} %fusion.20), kind=kLoop, calls=%fused_computation.8 | loop fusion | flops 1048576 | bytes 4194816 | tf_op jit(solution)/shard_map/while/body/eval_jaxpr/convert_element_type | solution.py:72
  (34 shorter events, 0.7 us)
Async XLA Ops:
  0.0 2.3 %copy-start.4 = (s32[512]{0:T(512)S(1)}, s32[512]{0:T(512)}, u32[]{:S(2)}) copy-start(s32[512]{0:T(512)} %param.14) | copy-start | bytes 6148
  0.0 4.0 %copy-start.5 = (f32[256]{0:T(256)S(1)}, f32[256]{0:T(256)}, u32[]{:S(2)}) copy-start(f32[256]{0:T(256)} %param.13) | copy-start | bytes 3076
  4.4 6.6 %copy-start.7 = (u32[32]{0:T(128)S(1)}, u32[32]{0:T(128)}, u32[]{:S(2)}) copy-start(u32[32]{0:T(128)} %constant.63) | copy-start | bytes 388
  4.8 98.1 %copy-start.1 = (bf16[512,4,256]{2,0,1:T(8,128)(2,1)}, bf16[512,4,256]{2,0,1:T(8,128)(2,1)S(1)}, u32[]{:S(2)}) copy-start(bf16[512,4,256]{2,0,1:T(8,128)(2,1)S(1)} %maximum_convert_fusion) | copy-start | bytes 3145732
  5.4 108.6 %collective-permute-start.2 = (bf16[512,1024]{0,1:T(8,128)(2,1)S(1)}, bf16[512,1024]{0,1:T(8,128)(2,1)}, u32[]{:S(2)}, u32[]{:S(2)}) collective-permute-start(bf16[512,1024]{0,1:T(8,128)(2,1)S(1)} %bitcast.54), channel_id=1, source_target_pairs={{0,2},{1,3},{2,4},{3,5},{4,6},{5,7},{6,8},{7,9},{8,10},{9,11},{10,... | collective-permute-start | bytes 3145736 | tf_op jit(solution)/shard_map/ppermute | solution.py:15
  6.7 109.6 %collective-permute-start.3 = (bf16[512,1024]{0,1:T(8,128)(2,1)S(1)}, bf16[512,1024]{0,1:T(8,128)(2,1)}, u32[]{:S(2)}, u32[]{:S(2)}) collective-permute-start(bf16[512,1024]{0,1:T(8,128)(2,1)S(1)} %bitcast.55), channel_id=1, source_target_pairs={{0,1},{1,2},{2,3},{3,4},{4,5},{5,6},{6,7},{7,8},{8,9},{9,10},{10,1... | collective-permute-start | bytes 3145736 | tf_op jit(solution)/shard_map/ppermute | solution.py:15
  8.0 110.6 %collective-permute-start = (bf16[512,1024]{1,0:T(8,128)(2,1)}, bf16[512,1024]{1,0:T(8,128)(2,1)}, u32[]{:S(2)}, u32[]{:S(2)}) collective-permute-start(bf16[512,1024]{1,0:T(8,128)(2,1)} %param.11), channel_id=1, source_target_pairs={{0,2},{1,3},{2,4},{3,5},{4,6},{5,7},{6,8},{7,9},{8,10},{9,11},{10,... | collective-permute-start | bytes 3145736 | tf_op jit(solution)/shard_map/ppermute | solution.py:15
  9.3 109.3 %collective-permute-start.1 = (bf16[512,1024]{1,0:T(8,128)(2,1)}, bf16[512,1024]{1,0:T(8,128)(2,1)}, u32[]{:S(2)}, u32[]{:S(2)}) collective-permute-start(bf16[512,1024]{1,0:T(8,128)(2,1)} %param.11), channel_id=1, source_target_pairs={{0,1},{1,2},{2,3},{3,4},{4,5},{5,6},{6,7},{7,8},{8,9},{9,10},{10,1... | collective-permute-start | bytes 3145736 | tf_op jit(solution)/shard_map/ppermute | solution.py:15
  102.9 1.9 %copy-start = (f32[64,8,8,256]{3,2,1,0:T(8,128)}, f32[64,8,8,256]{3,2,1,0:T(8,128)S(1)}, u32[]{:S(2)}) copy-start(f32[64,8,8,256]{3,2,1,0:T(8,128)S(1)} %copy.46) | copy-start | bytes 12582916
  102.9 2.8 %copy-start.6 = (f32[256]{0:T(256)S(1)}, f32[256]{0:T(256)}, u32[]{:S(2)}) copy-start(f32[256]{0:T(256)} %param.12) | copy-start | bytes 3076
  123.7 13.3 %copy-start.2 = (bf16[1536,1024]{0,1:T(8,128)(2,1)S(1)}, bf16[1536,1024]{0,1:T(8,128)(2,1)}, u32[]{:S(2)}) copy-start(bf16[1536,1024]{0,1:T(8,128)(2,1)} %copy.31) | copy-start | bytes 9437188
  123.7 13.3 %copy-start.3 = (pred[512,1536]{0,1:T(8,128)(4,1)S(1)}, pred[512,1536]{0,1:T(8,128)(4,1)}, u32[]{:S(2)}) copy-start(pred[512,1536]{0,1:T(8,128)(4,1)} %compare_and_fusion) | copy-start | bytes 2359300
where the time goes:
time: 154 us; the launch traced here: 153 us
  blocking collectives  66.7 us (43%)
  local copies, waits for them, and re-layouts  31.9 us (21%)
  matrix products  25.1 us (16%)
  other arithmetic  12.7 us (8%)
  loops' own time  11 us (7%)
  starting transfers between devices  5.17 us (3%)
    unnamed x1, blocking collectives  66.7 us
    dot_general x1, matrix products, attend(): jnp.einsum('qhgd,khd->hgqk', grouped_heads, key_head_split, preferred_ele...  13.3 us
    dot_general x1, matrix products, attend(): jnp.einsum('hgqk,khd->qhgd', rounded, value_head_split, preferred_element...  11.7 us
    another operation x1, loops' own time, prefix(): return lax.fori_loop(0, place, one, state)  11 us
    dynamic_slice x15, local copies, waits for them, and re-layouts, one(): return combine(state, lax.dynamic_index_in_dim(gathered, lap, 0, False))  10 us
    unnamed x21, local copies, waits for them, and re-layouts  7.58 us
    concatenate x3, local copies, waits for them, and re-layouts, body(): jnp.concatenate([portion[member] for portion in portions] + [payload[memb...  7.53 us
    ppermute x4, starting transfers between devices, shifted(): return lax.ppermute(array, axis, pairs)  5.17 us
  transfers between devices with their start and end apart: 4, of which 0 were waited for; matrix products, arithmetic and copies ran while one was open for 18% of the time, Pallas kernels for 0%

commit v1 on v0

v1 whole, which is shorter than its diff:
```python
import functools

import jax
import jax.numpy as jnp
import numpy as np
from jax import lax
from jax.experimental import pallas as pl
from jax.experimental.pallas import tpu as pltpu
from jax.sharding import PartitionSpec as P

QUERY_HEADS = 8
KEY_VALUE_HEADS = 4
HEAD = 256
HALF = HEAD // 2
WINDOW = 1024
ROWS = 512
SUB = 256
MESH = pl.DeviceIdType.MESH


def kernel(
    count,
    q_hbm,
    k_hbm,
    v_hbm,
    gains_ref,
    flags_ref,
    limit_ref,
    rope_hbm,
    inverse_ref,
    o_hbm,
    q_in,
    k_in,
    rope,
    kbuf,
    vbuf,
    ksend,
    qbuf,
    qsend,
    flags,
    low,
    acc,
    total,
    stage,
    load_sem,
    vloc_sem,
    fsend_sem,
    frecv_sem,
    pk_send,
    pk_recv,
    pv_send,
    pv_recv,
    k_send,
    k_recv,
    v_send,
    v_recv,
    q_send,
    q_recv,
    o_loc,
    o_send,
    o_recv,
):
    me = lax.axis_index("ctx")
    core = lax.rem(me, 2)
    other = 1 - core
    chip = me // 2
    chips = count // 2
    after = lax.rem(chip + 1, chips)
    before = lax.rem(chip + chips - 1, chips)
    partner = chip * 2 + other

    def span(index, width):
        return pl.ds(pl.multiple_of(index * width, width), width)

    def remote(src, dst, send, recv, target):
        return pltpu.make_async_remote_copy(
            src_ref=src,
            dst_ref=dst,
            send_sem=send,
            recv_sem=recv,
            device_id={"ctx": target},
            device_id_type=MESH,
        )

    load_k = pltpu.make_async_copy(k_hbm, k_in, load_sem.at[0])
    load_r = pltpu.make_async_copy(rope_hbm, rope, load_sem.at[1])
    load_q = pltpu.make_async_copy(q_hbm, q_in, load_sem.at[2])
    load_k.start()
    load_r.start()
    load_q.start()
    own_rows = span(2 + core, ROWS)
    v_local = [
        pltpu.make_async_copy(
            v_hbm.at[:, span(core * 2 + h, HEAD)], vbuf.at[h, own_rows], vloc_sem.at[h]
        )
        for h in range(2)
    ]
    for copy in v_local:
        copy.start()
    flags[2 + core] = jnp.broadcast_to(flags_ref[...], (8, ROWS))

    barrier = pltpu.get_barrier_semaphore()
    for target in (before * 2, before * 2 + 1, after * 2, after * 2 + 1, partner):
        pl.semaphore_signal(barrier, inc=1, device_id={"ctx": target}, device_id_type=MESH)
    pl.semaphore_wait(barrier, 5)

    near, far = after * 2 + core, after * 2 + other
    flag_out = [
        remote(flags.at[2 + core], flags.at[2 + core], fsend_sem.at[0], frecv_sem.at[2], partner),
        remote(flags.at[2 + core], flags.at[core], fsend_sem.at[1], frecv_sem.at[core], near),
        remote(flags.at[2 + core], flags.at[core], fsend_sem.at[2], frecv_sem.at[core], far),
    ]
    for copy in flag_out:
        copy.start()

    there = span(core, ROWS)
    v_out = []
    for h in range(2):
        mine = v_hbm.at[:, span(core * 2 + h, HEAD)]
        theirs = v_hbm.at[:, span(other * 2 + h, HEAD)]
        v_out += [
            remote(mine, vbuf.at[h, there], v_send.at[h, 0], v_recv.at[h, core], near),
            remote(theirs, vbuf.at[h, there], v_send.at[h, 1], v_recv.at[h, core], far),
        ]
    for copy in v_out:
        copy.start()
    pv_out = [
        remote(
            v_hbm.at[:, span(other * 2 + h, HEAD)],
            vbuf.at[h, own_rows],
            pv_send.at[h],
            pv_recv.at[h],
            partner,
        )
        for h in range(2)
    ]

    device_start = me * ROWS
    base = device_start.astype(jnp.float32) * inverse_ref[...]
    base_cos, base_sin = jnp.cos(base)[:1], jnp.sin(base)[:1]
    load_r.wait()
    row_cos, row_sin = rope[0], rope[1]
    rope[0] = base_cos * row_cos - base_sin * row_sin
    rope[1] = base_sin * row_cos + base_cos * row_sin

    def normed(raw, gain, scale):
        x = raw.astype(jnp.float32)
        mean = jnp.sum(x * x, axis=-1, keepdims=True) * (1.0 / HEAD)
        x = x * lax.rsqrt(mean + 1e-06) * gain
        a, b = x[:, :HALF], x[:, HALF:]
        cosine, sine = rope[0], rope[1]
        first = (a * cosine - b * sine).astype(jnp.bfloat16)
        second = (b * cosine + a * sine).astype(jnp.bfloat16)
        if scale != 1.0:
            first, second = first * jnp.bfloat16(scale), second * jnp.bfloat16(scale)
        return first, second

    load_k.wait()
    k_out, pk_out = [], []
    for h in range(2):
        first, second = normed(k_in[:, span(core * 2 + h, HEAD)], gains_ref[1:2], 1.0)
        kbuf[h, own_rows, :HALF] = first
        kbuf[h, own_rows, HALF:] = second
        first, second = normed(k_in[:, span(other * 2 + h, HEAD)], gains_ref[1:2], 1.0)
        ksend[h, :, :HALF] = first
        ksend[h, :, HALF:] = second
        pair = [
            remote(kbuf.at[h, own_rows], kbuf.at[h, there], k_send.at[h, 0], k_recv.at[h, core], near),
            remote(ksend.at[h], kbuf.at[h, there], k_send.at[h, 1], k_recv.at[h, core], far),
        ]
        for copy in pair:
            copy.start()
        k_out += pair
        pk_out.append(
            remote(ksend.at[h], kbuf.at[h, own_rows], pk_send.at[h], pk_recv.at[h], partner)
        )
        pk_out[-1].start()
        pv_out[h].start()

    load_q.wait()
    mine_rows = span(core, ROWS)
    q_out = []
    for j in range(4):
        first, second = normed(q_in[:, span(other * 4 + j, HEAD)], gains_ref[0:1], HEAD**-0.5)
        qsend[j, :, :HALF] = first
        qsend[j, :, HALF:] = second
        q_out.append(
            remote(qsend.at[j], qbuf.at[j // 2, j % 2, mine_rows], q_send.at[j], q_recv.at[j], partner)
        )
        q_out[-1].start()
    for j in range(4):
        first, second = normed(q_in[:, span(core * 4 + j, HEAD)], gains_ref[0:1], HEAD**-0.5)
        qbuf[j // 2, j % 2, mine_rows, :HALF] = first
        qbuf[j // 2, j % 2, mine_rows, HALF:] = second

    remote(flags.at[0], flags.at[2 + other], fsend_sem.at[0], frecv_sem.at[2], partner).wait_recv()
    for s in range(2):
        remote(flags.at[0], flags.at[s], fsend_sem.at[0], frecv_sem.at[s], partner).wait_recv()
    first_tick = (chip * 2 - 2) * ROWS
    column = lax.broadcasted_iota(jnp.int32, (8, ROWS), 1)

    def marks(slot):
        place = column + slot * ROWS
        return jnp.where((flags[slot] == 1) & (place + first_tick >= 0), place, -first_tick)

    behind = jnp.max(jnp.maximum(marks(0), marks(1)), axis=1, keepdims=True)[:1]
    row = lax.broadcasted_iota(jnp.int32, (ROWS, ROWS), 0)
    col = lax.broadcasted_iota(jnp.int32, (ROWS, ROWS), 1)
    for b in range(2):
        line = marks(2 + b)[:1]
        seen = jnp.where(col <= row, jnp.broadcast_to(line, (ROWS, ROWS)), -first_tick)
        start = jnp.maximum(jnp.max(seen, axis=1, keepdims=True), behind)
        behind = jnp.maximum(behind, jnp.max(line, axis=1, keepdims=True))
        tick = lax.broadcasted_iota(jnp.int32, (ROWS, 1), 0) + (2 + b) * ROWS
        start = jnp.maximum(start, tick - (WINDOW - 1))
        low[pl.ds(b * ROWS, ROWS)] = jnp.broadcast_to(start, (ROWS, 128))

    def part(h, u, key_first, keys, first_use):
        ticks = pl.ds(u * SUB, SUB)
        q = qbuf[h, :, ticks, :].reshape(2 * SUB, HEAD)
        k = kbuf[h, pl.ds(key_first, keys), :]
        v = vbuf[h, pl.ds(key_first, keys), :]
        score = lax.dot_general(q, k, (((1,), (1,)), ((), ())), preferred_element_type=jnp.float32)
        place = lax.broadcasted_iota(jnp.int32, (SUB, keys), 1) + key_first
        allowed = place >= low[ticks][:, :1]
        if key_first + keys > WINDOW + u * SUB:
            tick = lax.broadcasted_iota(jnp.int32, (SUB, keys), 0) + (WINDOW + u * SUB)
            allowed = allowed & (place <= tick)
        weight = jnp.where(allowed[None], jnp.exp(score).reshape(2, SUB, keys), 0.0)
        weight = weight.reshape(2 * SUB, keys)
        lanes = weight[:, :128]
        for i in range(1, keys // 128):
            lanes = lanes + weight[:, i * 128 : (i + 1) * 128]
        mixed = jnp.dot(weight.astype(jnp.bfloat16), v, preferred_element_type=jnp.float32)
        if first_use:
            acc[h, u] = mixed
            total[h, u] = lanes
        else:
            acc[h, u] += mixed
            total[h, u] += lanes

    for copy in v_local:
        copy.wait()
    for j in range(4):
        remote(qsend.at[j], qbuf.at[j // 2, j % 2, span(other, ROWS)], q_send.at[j], q_recv.at[j], partner).wait_recv()

    partner_rows = span(2 + other, ROWS)

    def own(h, carry):
        remote(ksend.at[0], kbuf.at[h, partner_rows], pk_send.at[0], pk_recv.at[h], partner).wait_recv()
        remote(ksend.at[0], vbuf.at[h, partner_rows], pv_send.at[0], pv_recv.at[h], partner).wait_recv()
        part(h, 0, WINDOW, 256, True)
        part(h, 1, WINDOW, 512, True)
        part(h, 2, WINDOW, 512, True)
        part(h, 2, WINDOW + 512, 256, False)
        part(h, 3, WINDOW, 512, True)
        part(h, 3, WINDOW + 512, 512, False)
        return carry

    lax.fori_loop(0, 2, own, 0)

    limit = limit_ref[0]

    def finish(h, u):
        whole = jnp.sum(total[h, u], axis=-1, keepdims=True)
        value = (acc[h, u] / whole).reshape(2, SUB, HEAD)
        tick = lax.broadcasted_iota(jnp.int32, (SUB, HEAD), 0) + (first_tick + WINDOW + u * SUB)
        value = jnp.where((tick < limit)[None], value, 0.0).astype(jnp.bfloat16)
        stage[h, :, pl.ds(u * SUB, SUB), :] = value

    def out_copies(h, j):
        columns = span(core * 4 + h * 2 + j, HEAD)
        local = pltpu.make_async_copy(
            stage.at[h, j, mine_rows], o_hbm.at[:, columns], o_loc.at[h, j]
        )
        away = remote(
            stage.at[h, j, span(other, ROWS)],
            o_hbm.at[:, columns],
            o_send.at[h, j],
            o_recv.at[h, j],
            partner,
        )
        return local, away

    def far_keys(h, carry):
        for s in range(2):
            rows = pl.ds(s * ROWS, ROWS)
            remote(ksend.at[0], vbuf.at[h, rows], v_send.at[0, 0], v_recv.at[h, s], partner).wait_recv()
            remote(ksend.at[0], kbuf.at[h, rows], k_send.at[0, 0], k_recv.at[h, s], partner).wait_recv()
            if s == 0:
                part(h, 0, 0, 512, False)
                part(h, 1, 256, 256, False)
            else:
                part(h, 0, 512, 512, False)
                part(h, 1, 512, 512, False)
                part(h, 2, 512, 512, False)
                part(h, 3, 768, 256, False)
        for u in range(4):
            finish(h, u)
        for j in range(2):
            for copy in out_copies(h, j):
                copy.start()
        return carry

    lax.fori_loop(0, 2, far_keys, 0)

    for h in range(2):
        for j in range(2):
            local, away = out_copies(h, j)
            local.wait()
            away.wait_send()
            columns = span(other * 4 + h * 2 + j, HEAD)
            remote(stage.at[h, j, mine_rows], o_hbm.at[:, columns], o_send.at[h, j], o_recv.at[h, j], partner).wait_recv()
    for copy in flag_out + v_out + pv_out + k_out + pk_out + q_out:
        copy.wait_send()


def solution(mesh):
    count = mesh.shape["ctx"]
    inverse = 10000.0 ** (-(np.arange(HALF, dtype=np.float64) * (2.0 / HEAD)))
    angle = np.arange(ROWS, dtype=np.float64)[:, None] * inverse
    table = np.stack([np.cos(angle), np.sin(angle)]).astype(np.float32)

    def body(queries, keys, values, query_gain, key_gain, session_flags, valid_length):
        assert queries.shape[0] == ROWS and 2 * ROWS == WINDOW
        gains = jnp.stack([query_gain, key_gain])
        bf16, f32, i32 = jnp.bfloat16, jnp.float32, jnp.int32
        dma = pltpu.SemaphoreType.DMA
        anywhere = pl.BlockSpec(memory_space=pl.ANY)
        vmem = pl.BlockSpec(memory_space=pltpu.VMEM)
        smem = pl.BlockSpec(memory_space=pltpu.SMEM)
        return pl.pallas_call(
            functools.partial(kernel, count),
            out_shape=jax.ShapeDtypeStruct((ROWS, QUERY_HEADS * HEAD), bf16),
            in_specs=[anywhere, anywhere, anywhere, vmem, vmem, smem, anywhere, vmem],
            out_specs=anywhere,
            scratch_shapes=[
                pltpu.VMEM((ROWS, QUERY_HEADS * HEAD), bf16),
                pltpu.VMEM((ROWS, KEY_VALUE_HEADS * HEAD), bf16),
                pltpu.VMEM((2, ROWS, HALF), f32),
                pltpu.VMEM((2, 4 * ROWS, HEAD), bf16),
                pltpu.VMEM((2, 4 * ROWS, HEAD), bf16),
                pltpu.VMEM((2, ROWS, HEAD), bf16),
                pltpu.VMEM((2, 2, 2 * ROWS, HEAD), bf16),
                pltpu.VMEM((4, ROWS, HEAD), bf16),
                pltpu.VMEM((4, 8, ROWS), i32),
                pltpu.VMEM((2 * ROWS, 128), i32),
                pltpu.VMEM((2, 4, 2 * SUB, HEAD), f32),
                pltpu.VMEM((2, 4, 2 * SUB, 128), f32),
                pltpu.VMEM((2, 2, 2 * ROWS, HEAD), bf16),
                dma((3,)),
                dma((2,)),
                dma((3,)),
                dma((3,)),
                dma((2,)),
                dma((2,)),
                dma((2,)),
                dma((2,)),
                dma((2, 2)),
                dma((2, 2)),
                dma((2, 2)),
                dma((2, 2)),
                dma((4,)),
                dma((4,)),
                dma((2, 2)),
                dma((2, 2)),
                dma((2, 2)),
            ],
            compiler_params=pltpu.CompilerParams(
                collective_id=0, has_side_effects=True, vmem_limit_bytes=48 << 20
            ),
        )(
            queries,
            keys,
            values,
            gains,
            session_flags.reshape(1, ROWS),
            valid_length,
            jnp.asarray(table),
            jnp.asarray(np.broadcast_to(inverse.astype(np.float32), (8, HALF))),
        )

    return jax.shard_map(
        body,
        mesh=mesh,
        in_specs=(
            P(("dates", "ctx"), None),
            P(("dates", "ctx"), None),
            P(("dates", "ctx"), None),
            P(),
            P(),
            P(("dates", "ctx")),
            P("dates"),
        ),
        out_specs=P(("dates", "ctx"), None),
        check_vma=False,
    )
```

time: 154 us -> 65 us (0.42)
  the two profiles are of different devices: /device:TPU:27 before, /device:TPU:0 now
where the time goes in v1:
time: 65 us; the launch traced here: 64.7 us
  Pallas kernels  57.2 us (88%)
  local copies, waits for them, and re-layouts  6.15 us (9%)
  other arithmetic  0.7 us (1%)
  between operations  0.67 us (1%)
    pallas_call x1, Pallas kernels, body(): pl.pallas_call(functools.partial(kernel, count), out_shape=jax.ShapeDtype...  57.2 us
    unnamed x9, local copies, waits for them, and re-layouts  5.49 us

profile of v1, /device:TPU:0, one launch (start us, length us, event | category | flops | bytes accessed | tf_op | source)
XLA Modules:
  0.0 64.7 jit_solution(8159257947192415291)
XLA Ops:
  0.7 0.7 %pad_maximum_fusion.gains_ref = f32[2,256]{1,0:T(2,128)S(1)} fusion(f32[1,256]{1,0:T(1,128)} %bitcast.4, f32[1,256]{1,0:T(1,128)} %bitcast.5), kind=kLoop, calls=%fused_computation | loop fusion | flops 512 | bytes 4096 | tf_op jit(solution)/shard_map/stack | solution.py:326
  1.4 0.7 %jit_solution_.3.inverse_ref = f32[8,128]{1,0:T(8,128)S(1)} broadcast(f32[128]{0:T(128)} %constant.5.clone), dimensions={1} | broadcast | bytes 4608 | tf_op jit(solution)
  2.0 0.0 copy-start
  2.0 1.2 %copy-done = bf16[512,1024]{1,0:T(8,128)(2,1)S(1)} copy-done((bf16[512,1024]{1,0:T(8,128)(2,1)S(1)}, bf16[512,1024]{1,0:T(8,128)(2,1)}, u32[]{:S(2)}) %copy-start) | copy-done | bytes 1048600
  3.2 0.0 copy-start.1
  3.2 1.2 %copy-done.1 = bf16[512,1024]{1,0:T(8,128)(2,1)S(1)} copy-done((bf16[512,1024]{1,0:T(8,128)(2,1)S(1)}, bf16[512,1024]{1,0:T(8,128)(2,1)}, u32[]{:S(2)}) %copy-start.1) | copy-done | bytes 1048600
  4.5 0.0 copy-start.2
  4.5 1.0 %copy-done.2 = f32[2,512,128]{2,1,0:T(8,128)S(1)} copy-done((f32[2,512,128]{2,1,0:T(8,128)S(1)}, f32[2,512,128]{2,1,0:T(8,128)}, u32[]{:S(2)}) %copy-start.2) | copy-done | bytes 524312
  5.5 0.0 copy-start.3
  5.5 0.7 %copy-done.3 = s32[512]{0:T(512)S(1)} copy-done((s32[512]{0:T(512)S(1)}, s32[512]{0:T(512)}, u32[]{:S(2)}) %copy-start.3) | copy-done | bytes 2072
  6.2 57.2 %shard_map.91 = bf16[512,2048]{1,0:T(8,128)(2,1)S(1)} custom-call(bf16[512,2048]{1,0:T(8,128)(2,1)} %q_hbm.1, bf16[512,1024]{1,0:T(8,128)(2,1)S(1)} %copy-done, bf16[512,1024]{1,0:T(8,128)(2,1)S(1)} %copy-done.1, f32[2,256]{1,0:T(2,128)S(1)} %pad_maximum_fusion.gains_ref, s32[1,512]{1,0:T(1,128)S(1)} %bitcast.3, s32[1]{0:T(128)S(6)} %copy.11.limit_ref, ...), custom_call_target="tpu_custom_call" | custom-call | tf_op jit(solution)/shard_map/pallas_call | solution.py:332
  63.4 1.3 %copy.12 = bf16[512,2048]{1,0:T(8,128)(2,1)} copy(bf16[512,2048]{1,0:T(8,128)(2,1)S(1)} %shard_map.91) | data formatting | bytes 4194304
Async XLA Ops:
  2.0 1.2 %copy-start = (bf16[512,1024]{1,0:T(8,128)(2,1)S(1)}, bf16[512,1024]{1,0:T(8,128)(2,1)}, u32[]{:S(2)}) copy-start(bf16[512,1024]{1,0:T(8,128)(2,1)} %k_hbm.1) | copy-start | bytes 3145732
  3.2 1.2 %copy-start.1 = (bf16[512,1024]{1,0:T(8,128)(2,1)S(1)}, bf16[512,1024]{1,0:T(8,128)(2,1)}, u32[]{:S(2)}) copy-start(bf16[512,1024]{1,0:T(8,128)(2,1)} %v_hbm.1) | copy-start | bytes 3145732
  4.5 1.0 %copy-start.2 = (f32[2,512,128]{2,1,0:T(8,128)S(1)}, f32[2,512,128]{2,1,0:T(8,128)}, u32[]{:S(2)}) copy-start(f32[2,512,128]{2,1,0:T(8,128)} %constant.4.clone.rope_hbm) | copy-start | bytes 1572868
  5.5 0.7 %copy-start.3 = (s32[512]{0:T(512)S(1)}, s32[512]{0:T(512)}, u32[]{:S(2)}) copy-start(s32[512]{0:T(512)} %param.14) | copy-start | bytes 6148

commit v2 on v1

--- a/solution.py
+++ b/solution.py
@@ -23,11 +23,10 @@
     q_hbm,
     k_hbm,
     v_hbm,
-    gains_ref,
+    q_gain,
+    k_gain,
     flags_ref,
-    limit_ref,
     rope_hbm,
-    inverse_ref,
     o_hbm,
     q_in,
     k_in,
@@ -42,6 +41,7 @@
     acc,
     total,
     stage,
+    held,
     load_sem,
     vloc_sem,
     fsend_sem,
@@ -122,7 +122,7 @@
             remote(mine, vbuf.at[h, there], v_send.at[h, 0], v_recv.at[h, core], near),
             remote(theirs, vbuf.at[h, there], v_send.at[h, 1], v_recv.at[h, core], far),
         ]
-    for copy in v_out:
+    for copy in v_out[:2]:
         copy.start()
     pv_out = [
         remote(
@@ -136,9 +136,9 @@
     ]
 
     device_start = me * ROWS
-    base = device_start.astype(jnp.float32) * inverse_ref[...]
+    load_r.wait()
+    base = device_start.astype(jnp.float32) * rope[2, :8]
     base_cos, base_sin = jnp.cos(base)[:1], jnp.sin(base)[:1]
-    load_r.wait()
     row_cos, row_sin = rope[0], rope[1]
     rope[0] = base_cos * row_cos - base_sin * row_sin
     rope[1] = base_sin * row_cos + base_cos * row_sin
@@ -158,10 +158,10 @@
     load_k.wait()
     k_out, pk_out = [], []
     for h in range(2):
-        first, second = normed(k_in[:, span(core * 2 + h, HEAD)], gains_ref[1:2], 1.0)
+        first, second = normed(k_in[:, span(core * 2 + h, HEAD)], k_gain[...], 1.0)
         kbuf[h, own_rows, :HALF] = first
         kbuf[h, own_rows, HALF:] = second
-        first, second = normed(k_in[:, span(other * 2 + h, HEAD)], gains_ref[1:2], 1.0)
+        first, second = normed(k_in[:, span(other * 2 + h, HEAD)], k_gain[...], 1.0)
         ksend[h, :, :HALF] = first
         ksend[h, :, HALF:] = second
         pair = [
@@ -174,6 +174,9 @@
         pk_out.append(
             remote(ksend.at[h], kbuf.at[h, own_rows], pk_send.at[h], pk_recv.at[h], partner)
         )
+        if h == 1:
+            for copy in v_out[2:]:
+                copy.start()
         pk_out[-1].start()
         pv_out[h].start()
 
@@ -181,7 +184,7 @@
     mine_rows = span(core, ROWS)
     q_out = []
     for j in range(4):
-        first, second = normed(q_in[:, span(other * 4 + j, HEAD)], gains_ref[0:1], HEAD**-0.5)
+        first, second = normed(q_in[:, span(other * 4 + j, HEAD)], q_gain[...], HEAD**-0.5)
         qsend[j, :, :HALF] = first
         qsend[j, :, HALF:] = second
         q_out.append(
@@ -189,7 +192,7 @@
         )
         q_out[-1].start()
     for j in range(4):
-        first, second = normed(q_in[:, span(core * 4 + j, HEAD)], gains_ref[0:1], HEAD**-0.5)
+        first, second = normed(q_in[:, span(core * 4 + j, HEAD)], q_gain[...], HEAD**-0.5)
         qbuf[j // 2, j % 2, mine_rows, :HALF] = first
         qbuf[j // 2, j % 2, mine_rows, HALF:] = second
 
@@ -215,11 +218,10 @@
         start = jnp.maximum(start, tick - (WINDOW - 1))
         low[pl.ds(b * ROWS, ROWS)] = jnp.broadcast_to(start, (ROWS, 128))
 
-    def part(h, u, key_first, keys, first_use):
+    def weigh(h, u, key_first, keys):
         ticks = pl.ds(u * SUB, SUB)
         q = qbuf[h, :, ticks, :].reshape(2 * SUB, HEAD)
         k = kbuf[h, pl.ds(key_first, keys), :]
-        v = vbuf[h, pl.ds(key_first, keys), :]
         score = lax.dot_general(q, k, (((1,), (1,)), ((), ())), preferred_element_type=jnp.float32)
         place = lax.broadcasted_iota(jnp.int32, (SUB, keys), 1) + key_first
         allowed = place >= low[ticks][:, :1]
@@ -231,7 +233,12 @@
         lanes = weight[:, :128]
         for i in range(1, keys // 128):
             lanes = lanes + weight[:, i * 128 : (i + 1) * 128]
-        mixed = jnp.dot(weight.astype(jnp.bfloat16), v, preferred_element_type=jnp.float32)
+        return weight.astype(jnp.bfloat16), lanes
+
+    def part(h, u, key_first, keys, first_use):
+        weight, lanes = weigh(h, u, key_first, keys)
+        v = vbuf[h, pl.ds(key_first, keys), :]
+        mixed = jnp.dot(weight, v, preferred_element_type=jnp.float32)
         if first_use:
             acc[h, u] = mixed
             total[h, u] = lanes
@@ -259,14 +266,10 @@
 
     lax.fori_loop(0, 2, own, 0)
 
-    limit = limit_ref[0]
-
     def finish(h, u):
         whole = jnp.sum(total[h, u], axis=-1, keepdims=True)
         value = (acc[h, u] / whole).reshape(2, SUB, HEAD)
-        tick = lax.broadcasted_iota(jnp.int32, (SUB, HEAD), 0) + (first_tick + WINDOW + u * SUB)
-        value = jnp.where((tick < limit)[None], value, 0.0).astype(jnp.bfloat16)
-        stage[h, :, pl.ds(u * SUB, SUB), :] = value
+        stage[h, :, pl.ds(u * SUB, SUB), :] = value.astype(jnp.bfloat16)
 
     def out_copies(h, j):
         columns = span(core * 4 + h * 2 + j, HEAD)
@@ -282,27 +285,51 @@
         )
         return local, away
 
-    def far_keys(h, carry):
-        for s in range(2):
-            rows = pl.ds(s * ROWS, ROWS)
-            remote(ksend.at[0], vbuf.at[h, rows], v_send.at[0, 0], v_recv.at[h, s], partner).wait_recv()
-            remote(ksend.at[0], kbuf.at[h, rows], k_send.at[0, 0], k_recv.at[h, s], partner).wait_recv()
-            if s == 0:
-                part(h, 0, 0, 512, False)
-                part(h, 1, 256, 256, False)
-            else:
-                part(h, 0, 512, 512, False)
-                part(h, 1, 512, 512, False)
-                part(h, 2, 512, 512, False)
-                part(h, 3, 768, 256, False)
+    def arrived(buffer, h, s, sems):
+        remote(ksend.at[0], buffer.at[h, pl.ds(s * ROWS, ROWS)], k_send.at[0, 0], sems.at[h, s], partner).wait_recv()
+
+    for s in range(2):
+        arrived(vbuf, 0, s, v_recv)
+        arrived(kbuf, 0, s, k_recv)
+        if s == 0:
+            part(0, 0, 0, 512, False)
+            part(0, 1, 256, 256, False)
+        else:
+            for u in range(4):
+                part(0, u, max(512, u * SUB), WINDOW - max(512, u * SUB), False)
+    for u in range(4):
+        finish(0, u)
+    for j in range(2):
+        for copy in out_copies(0, j):
+            copy.start()
+
+    for s in range(2):
+        arrived(kbuf, 1, s, k_recv)
         for u in range(4):
-            finish(h, u)
+            first, last = max(s * ROWS, u * SUB), (s + 1) * ROWS
+            if first < last:
+                weight, lanes = weigh(1, u, first, last - first)
+                held[u, :, pl.ds(first, last - first)] = weight
+                total[1, u] += lanes
+    for s in range(2):
+        arrived(vbuf, 1, s, v_recv)
+
+    def mix(block):
+        for u in (2 * block, 2 * block + 1):
+            keys = pl.ds(u * SUB, WINDOW - u * SUB)
+            acc[1, u] += jnp.dot(held[u, :, keys], vbuf[1, keys, :], preferred_element_type=jnp.float32)
+            finish(1, u)
+
+    def last_tiles(first_block):
+        mix(first_block)
         for j in range(2):
-            for copy in out_copies(h, j):
-                copy.start()
-        return carry
-
-    lax.fori_loop(0, 2, far_keys, 0)
+            out_copies(1, j)[1].start()
+        mix(1 - first_block)
+
+    pl.when(core == 0)(lambda: last_tiles(1))
+    pl.when(core == 1)(lambda: last_tiles(0))
+    for j in range(2):
+        out_copies(1, j)[0].start()
 
     for h in range(2):
         for j in range(2):
@@ -319,25 +346,24 @@
     count = mesh.shape["ctx"]
     inverse = 10000.0 ** (-(np.arange(HALF, dtype=np.float64) * (2.0 / HEAD)))
     angle = np.arange(ROWS, dtype=np.float64)[:, None] * inverse
-    table = np.stack([np.cos(angle), np.sin(angle)]).astype(np.float32)
+    table = np.stack([np.cos(angle), np.sin(angle), 0 * angle + inverse]).astype(np.float32)
 
     def body(queries, keys, values, query_gain, key_gain, session_flags, valid_length):
         assert queries.shape[0] == ROWS and 2 * ROWS == WINDOW
-        gains = jnp.stack([query_gain, key_gain])
+        pinned = functools.partial(pltpu.with_memory_space_constraint, memory_space=pltpu.HBM)
         bf16, f32, i32 = jnp.bfloat16, jnp.float32, jnp.int32
         dma = pltpu.SemaphoreType.DMA
-        anywhere = pl.BlockSpec(memory_space=pl.ANY)
+        anywhere = pl.BlockSpec(memory_space=pltpu.HBM)
         vmem = pl.BlockSpec(memory_space=pltpu.VMEM)
-        smem = pl.BlockSpec(memory_space=pltpu.SMEM)
-        return pl.pallas_call(
+        mixed = pl.pallas_call(
             functools.partial(kernel, count),
-            out_shape=jax.ShapeDtypeStruct((ROWS, QUERY_HEADS * HEAD), bf16),
-            in_specs=[anywhere, anywhere, anywhere, vmem, vmem, smem, anywhere, vmem],
-            out_specs=anywhere,
+            out_shape=pltpu.VMEM((ROWS, QUERY_HEADS * HEAD), bf16),
+            in_specs=[anywhere, anywhere, anywhere, vmem, vmem, vmem, anywhere],
+            out_specs=pl.BlockSpec(memory_space=pl.ANY),
             scratch_shapes=[
                 pltpu.VMEM((ROWS, QUERY_HEADS * HEAD), bf16),
                 pltpu.VMEM((ROWS, KEY_VALUE_HEADS * HEAD), bf16),
-                pltpu.VMEM((2, ROWS, HALF), f32),
+                pltpu.VMEM((3, ROWS, HALF), f32),
                 pltpu.VMEM((2, 4 * ROWS, HEAD), bf16),
                 pltpu.VMEM((2, 4 * ROWS, HEAD), bf16),
                 pltpu.VMEM((2, ROWS, HEAD), bf16),
@@ -348,6 +374,7 @@
                 pltpu.VMEM((2, 4, 2 * SUB, HEAD), f32),
                 pltpu.VMEM((2, 4, 2 * SUB, 128), f32),
                 pltpu.VMEM((2, 2, 2 * ROWS, HEAD), bf16),
+                pltpu.VMEM((4, 2 * SUB, WINDOW), bf16),
                 dma((3,)),
                 dma((2,)),
                 dma((3,)),
@@ -367,18 +394,19 @@
                 dma((2, 2)),
             ],
             compiler_params=pltpu.CompilerParams(
-                collective_id=0, has_side_effects=True, vmem_limit_bytes=48 << 20
+                collective_id=0, has_side_effects=True, vmem_limit_bytes=60 << 20
             ),
         )(
-            queries,
-            keys,
-            values,
-            gains,
+            pinned(queries),
+            pinned(keys),
+            pinned(values),
+            query_gain.reshape(1, HEAD),
+            key_gain.reshape(1, HEAD),
             session_flags.reshape(1, ROWS),
-            valid_length,
-            jnp.asarray(table),
-            jnp.asarray(np.broadcast_to(inverse.astype(np.float32), (8, HALF))),
-        )
+            pinned(jnp.asarray(table)),
+        )
+        tick = lax.axis_index("ctx") * ROWS + lax.broadcasted_iota(i32, mixed.shape, 0)
+        return jnp.where(tick < valid_length[0], mixed, jnp.zeros((), bf16))
 
     return jax.shard_map(
         body,

time: 65 us -> 58.7 us (0.903)
  local copies, waits for them, and re-layouts: 6.15 us -> 0 us
  other arithmetic: 0.7 us -> 1.54 us
  Pallas kernels: 57.2 us -> 56.4 us
    unnamed x9 -> x0, local copies, waits for them, and re-layouts: 5.49 us -> none
    select_n x0 -> x1, other arithmetic: none -> 1.53 us  [body(): return jnp.where(tick < valid_length[0], mixed, jnp.zeros((), bf16))]
    pallas_call x1, Pallas kernels: 57.2 us -> 56.4 us  [body(): pl.pallas_call(functools.partial(kernel, count), out_shape=pltpu.VMEM((RO...]
    another operation x1 -> x0, other arithmetic: 0.7 us -> none  [body(): gains = jnp.stack([query_gain, key_gain])]
    another operation x1 -> x0, local copies, waits for them, and re-layouts: 0.66 us -> none
where the time goes in v2:
time: 58.7 us; the launch traced here: 58.6 us
  Pallas kernels  56.4 us (96%)
  other arithmetic  1.54 us (3%)
  between operations  0.67 us (1%)
    pallas_call x1, Pallas kernels, body(): pl.pallas_call(functools.partial(kernel, count), out_shape=pltpu.VMEM((RO...  56.4 us
    select_n x1, other arithmetic, body(): return jnp.where(tick < valid_length[0], mixed, jnp.zeros((), bf16))  1.53 us

profile of v2, /device:TPU:0, one launch (start us, length us, event | category | flops | bytes accessed | tf_op | source)
XLA Modules:
  0.0 58.6 jit_solution(4884725291638575114)
XLA Ops:
  0.7 56.4 %shard_map.82 = bf16[512,2048]{1,0:T(8,128)(2,1)S(1)} custom-call(bf16[512,2048]{1,0:T(8,128)(2,1)} %q_hbm.1, bf16[512,1024]{1,0:T(8,128)(2,1)} %k_hbm.1, bf16[512,1024]{1,0:T(8,128)(2,1)} %v_hbm.1, f32[1,256]{1,0:T(1,128)} %bitcast.6, f32[1,256]{1,0:T(1,128)} %bitcast.7, s32[1,512]{1,0:T(1,128)} %bitcast.5, f32[3,512,128]{2,1,0:T(8,128)} %constant.10.clone.rope_hbm), custom_call_target="tpu_custom_call" | custom-call | tf_op jit(solution)/shard_map/pallas_call | solution.py:358
  57.0 1.5 %broadcast_select_fusion = bf16[512,2048]{1,0:T(8,128)(2,1)} fusion(bf16[512,2048]{1,0:T(8,128)(2,1)S(1)} %shard_map.82, pred[512]{0:T(512)(128)(4,1)S(1)} %add_compare_fusion), kind=kLoop, calls=%fused_computation | loop fusion | flops 1048576 | bytes 4194816 | tf_op jit(solution)/shard_map/jit(_where)/select_n | solution.py:409
  (1 shorter events, 0.0 us)

commit v3 on v2

--- a/solution.py
+++ b/solution.py
@@ -68,6 +68,7 @@
     after = lax.rem(chip + 1, chips)
     before = lax.rem(chip + chips - 1, chips)
     partner = chip * 2 + other
+    has_after, has_before = chip < chips - 1, chip > 0
 
     def span(index, width):
         return pl.ds(pl.multiple_of(index * width, width), width)
@@ -100,9 +101,25 @@
     flags[2 + core] = jnp.broadcast_to(flags_ref[...], (8, ROWS))
 
     barrier = pltpu.get_barrier_semaphore()
-    for target in (before * 2, before * 2 + 1, after * 2, after * 2 + 1, partner):
+
+    def ready(target):
         pl.semaphore_signal(barrier, inc=1, device_id={"ctx": target}, device_id_type=MESH)
-    pl.semaphore_wait(barrier, 5)
+
+    @pl.when(has_before)
+    def _():
+        ready(before * 2)
+        ready(before * 2 + 1)
+
+    ready(partner)
+    pl.when(has_after)(lambda: pl.semaphore_wait(barrier, 3))
+    pl.when(jnp.logical_not(has_after))(lambda: pl.semaphore_wait(barrier, 1))
+
+    def start_all(copies):
+        @pl.when(has_after)
+        def _():
+            for copy in copies:
+                copy.start()
+
 
     near, far = after * 2 + core, after * 2 + other
     flag_out = [
@@ -110,8 +127,8 @@
         remote(flags.at[2 + core], flags.at[core], fsend_sem.at[1], frecv_sem.at[core], near),
         remote(flags.at[2 + core], flags.at[core], fsend_sem.at[2], frecv_sem.at[core], far),
     ]
-    for copy in flag_out:
-        copy.start()
+    flag_out[0].start()
+    start_all(flag_out[1:])
 
     there = span(core, ROWS)
     v_out = []
@@ -122,8 +139,7 @@
             remote(mine, vbuf.at[h, there], v_send.at[h, 0], v_recv.at[h, core], near),
             remote(theirs, vbuf.at[h, there], v_send.at[h, 1], v_recv.at[h, core], far),
         ]
-    for copy in v_out[:2]:
-        copy.start()
+    start_all(v_out[:2])
     pv_out = [
         remote(
             v_hbm.at[:, span(other * 2 + h, HEAD)],
@@ -168,15 +184,13 @@
             remote(kbuf.at[h, own_rows], kbuf.at[h, there], k_send.at[h, 0], k_recv.at[h, core], near),
             remote(ksend.at[h], kbuf.at[h, there], k_send.at[h, 1], k_recv.at[h, core], far),
         ]
-        for copy in pair:
-            copy.start()
+        start_all(pair)
         k_out += pair
         pk_out.append(
             remote(ksend.at[h], kbuf.at[h, own_rows], pk_send.at[h], pk_recv.at[h], partner)
         )
         if h == 1:
-            for copy in v_out[2:]:
-                copy.start()
+            start_all(v_out[2:])
         pk_out[-1].start()
         pv_out[h].start()
 
@@ -197,8 +211,17 @@
         qbuf[j // 2, j % 2, mine_rows, HALF:] = second
 
     remote(flags.at[0], flags.at[2 + other], fsend_sem.at[0], frecv_sem.at[2], partner).wait_recv()
-    for s in range(2):
-        remote(flags.at[0], flags.at[s], fsend_sem.at[0], frecv_sem.at[s], partner).wait_recv()
+
+    @pl.when(has_before)
+    def _():
+        for s in range(2):
+            remote(flags.at[0], flags.at[s], fsend_sem.at[0], frecv_sem.at[s], partner).wait_recv()
+
+    @pl.when(jnp.logical_not(has_before))
+    def _():
+        for s in range(2):
+            flags[s] = jnp.zeros((8, ROWS), jnp.int32)
+
     first_tick = (chip * 2 - 2) * ROWS
     column = lax.broadcasted_iota(jnp.int32, (8, ROWS), 1)
 
@@ -288,36 +311,45 @@
     def arrived(buffer, h, s, sems):
         remote(ksend.at[0], buffer.at[h, pl.ds(s * ROWS, ROWS)], k_send.at[0, 0], sems.at[h, s], partner).wait_recv()
 
-    for s in range(2):
-        arrived(vbuf, 0, s, v_recv)
-        arrived(kbuf, 0, s, k_recv)
-        if s == 0:
-            part(0, 0, 0, 512, False)
-            part(0, 1, 256, 256, False)
-        else:
-            for u in range(4):
-                part(0, u, max(512, u * SUB), WINDOW - max(512, u * SUB), False)
+    @pl.when(has_before)
+    def _():
+        for s in range(2):
+            arrived(vbuf, 0, s, v_recv)
+            arrived(kbuf, 0, s, k_recv)
+            if s == 0:
+                part(0, 0, 0, 512, False)
+                part(0, 1, 256, 256, False)
+            else:
+                for u in range(4):
+                    part(0, u, max(512, u * SUB), WINDOW - max(512, u * SUB), False)
+
     for u in range(4):
         finish(0, u)
     for j in range(2):
         for copy in out_copies(0, j):
             copy.start()
 
-    for s in range(2):
-        arrived(kbuf, 1, s, k_recv)
-        for u in range(4):
-            first, last = max(s * ROWS, u * SUB), (s + 1) * ROWS
-            if first < last:
-                weight, lanes = weigh(1, u, first, last - first)
-                held[u, :, pl.ds(first, last - first)] = weight
-                total[1, u] += lanes
-    for s in range(2):
-        arrived(vbuf, 1, s, v_recv)
+    @pl.when(has_before)
+    def _():
+        for s in range(2):
+            arrived(kbuf, 1, s, k_recv)
+            for u in range(4):
+                first, last = max(s * ROWS, u * SUB), (s + 1) * ROWS
+                if first < last:
+                    weight, lanes = weigh(1, u, first, last - first)
+                    held[u, :, pl.ds(first, last - first)] = weight
+                    total[1, u] += lanes
+        for s in range(2):
+            arrived(vbuf, 1, s, v_recv)
 
     def mix(block):
         for u in (2 * block, 2 * block + 1):
             keys = pl.ds(u * SUB, WINDOW - u * SUB)
-            acc[1, u] += jnp.dot(held[u, :, keys], vbuf[1, keys, :], preferred_element_type=jnp.float32)
+
+            @pl.when(has_before)
+            def _():
+                acc[1, u] += jnp.dot(held[u, :, keys], vbuf[1, keys, :], preferred_element_type=jnp.float32)
+
             finish(1, u)
 
     def last_tiles(first_block):
@@ -338,8 +370,13 @@
             away.wait_send()
             columns = span(other * 4 + h * 2 + j, HEAD)
             remote(stage.at[h, j, mine_rows], o_hbm.at[:, columns], o_send.at[h, j], o_recv.at[h, j], partner).wait_recv()
-    for copy in flag_out + v_out + pv_out + k_out + pk_out + q_out:
+    for copy in flag_out[:1] + pv_out + pk_out + q_out:
         copy.wait_send()
+
+    @pl.when(has_after)
+    def _():
+        for copy in flag_out[1:] + v_out + k_out:
+            copy.wait_send()
 
 
 def solution(mesh):

time: 58.7 us -> 55.9 us (0.952)
  the two profiles are of different devices: /device:TPU:0 before, /device:TPU:13 now
where the time goes in v3:
time: 55.9 us; the launch traced here: 55.7 us
  Pallas kernels  53.5 us (96%)
  other arithmetic  1.54 us (3%)
  between operations  0.67 us (1%)
    pallas_call x1, Pallas kernels, body(): pl.pallas_call(functools.partial(kernel, count), out_shape=pltpu.VMEM((RO...  53.5 us
    select_n x1, other arithmetic, body(): return jnp.where(tick < valid_length[0], mixed, jnp.zeros((), bf16))  1.53 us

profile of v3, /device:TPU:13, one launch (start us, length us, event | category | flops | bytes accessed | tf_op | source)
XLA Modules:
  0.0 55.7 jit_solution(5663374705071842817)
XLA Ops:
  0.7 53.5 %shard_map.82 = bf16[512,2048]{1,0:T(8,128)(2,1)S(1)} custom-call(bf16[512,2048]{1,0:T(8,128)(2,1)} %q_hbm.1, bf16[512,1024]{1,0:T(8,128)(2,1)} %k_hbm.1, bf16[512,1024]{1,0:T(8,128)(2,1)} %v_hbm.1, f32[1,256]{1,0:T(1,128)} %bitcast.6, f32[1,256]{1,0:T(1,128)} %bitcast.7, s32[1,512]{1,0:T(1,128)} %bitcast.5, f32[3,512,128]{2,1,0:T(8,128)} %constant.10.clone.rope_hbm), custom_call_target="tpu_custom_call" | custom-call | tf_op jit(solution)/shard_map/pallas_call | solution.py:395
  54.1 1.5 %broadcast_select_fusion = bf16[512,2048]{1,0:T(8,128)(2,1)} fusion(bf16[512,2048]{1,0:T(8,128)(2,1)S(1)} %shard_map.82, pred[512]{0:T(512)(128)(4,1)S(1)} %add_compare_fusion), kind=kLoop, calls=%fused_computation | loop fusion | flops 1048576 | bytes 4194816 | tf_op jit(solution)/shard_map/jit(_where)/select_n | solution.py:446
  (1 shorter events, 0.0 us)
